TPU v7x, 256 devices: a whole 4x4x8 slice. The times are simulated.
256 devices in a mesh: seq: 32 (over z, y), dp: 8 (over x, core).
Axes of the slice: x: 4, y: 4, z: 8, core: 2. Of those that a mesh axis runs over, the one named last changes fastest.
Arguments:
- queries: bfloat16 [8, 4096, 4096], P('dp', 'seq'), may hold values from -118 to 118
- keys: bfloat16 [8, 4096, 1024], P('dp', 'seq'), may hold values from -9 to 9
- hidden: bfloat16 [8, 4096, 4096], P('dp', 'seq'), may hold values from -6 to 6
- value_weight: bfloat16 [4096, 1024], P('dp'), may hold values from -0.09375 to 0.09375
- readout: bfloat16 [4096, 256], replicated, may hold values from -1.796875 to 1.796875
- base_logits: float32 [8, 4096, 256], P('dp', 'seq'), may hold values from -12 to 300
- labels: int32 [8, 4096], P('dp', 'seq'), may hold values from 0 to 255
- hessian: float32 [1024, 4096], P('seq', 'dp'), may hold values from 0.05 to 2
Outputs:
- estimate: float32 [1024, 4096], P('seq', 'dp')
- hessian_new: float32 [1024, 4096], P('seq', 'dp')
All inputs are finite; a program needn't handle non-finite values.
Results may differ from a plain program's by a relative error of at most 0.033.
Values may be sent and summed in bfloat16 or wider, within the bound.
A program may use at most 64 MiB of HBM per device.

v0:
```python
import math
import jax
import jax.numpy as jnp
from jax import lax
from jax.sharding import PartitionSpec as P

HD = 128
big_negative = -1e30
beta_two = 0.99


def in_blocks(x, dim, count):
    before, after = (x.shape[:dim], x.shape[dim + 1 :])
    return jnp.moveaxis(x.reshape(*before, count, -1, *after), dim, 0)


def sum_at_owner(x, axis, dim):
    blocks = in_blocks(x, dim, lax.axis_size(axis))
    arrived = lax.all_to_all(blocks, axis, split_axis=0, concat_axis=0, tiled=True)
    return arrived.astype(jnp.float32).sum(axis=0)


def cut_rows(length, count):
    turn = length // count
    if turn >= 8:
        turn -= turn % 8
    return [turn * k for k in range(1, count)]


def in_order(blocks, dim):
    shape = list(blocks.shape[1:])
    shape[dim] *= blocks.shape[0]
    return jnp.moveaxis(blocks, 0, dim).reshape(shape)


def several_exchanges(x, axis, pieces, split_dim, concat_dim):
    blocks = in_blocks(x, split_dim, lax.axis_size(axis))
    cut = max(range(1, max(2, blocks.ndim - 1)), key=lambda d: blocks.shape[d])
    done = []
    for share in jnp.split(blocks, cut_rows(blocks.shape[cut], pieces), axis=cut):
        if share.size:
            done.append(lax.all_to_all(share, axis, split_axis=0, concat_axis=0, tiled=True))
    return in_order(jnp.concatenate(done, axis=cut), concat_dim)


def sent_to_all(x, axis):
    copies = jnp.broadcast_to(x, (lax.axis_size(axis), *x.shape))
    return lax.all_to_all(copies, axis, split_axis=0, concat_axis=0, tiled=True)


def collect(x, axis, dim):
    return in_order(sent_to_all(x, axis), dim)


def block_scores(q_block, k_block, row_start, col_start, scale):
    scores = (
        jnp.einsum("hqd,hkd->hqk", q_block, k_block, preferred_element_type=jnp.float32) * scale
    )
    rows_pos = row_start + lax.broadcasted_iota(jnp.int32, scores.shape, 1)
    cols_pos = col_start + lax.broadcasted_iota(jnp.int32, scores.shape, 2)
    return jnp.where(cols_pos <= rows_pos, scores, big_negative)


def row_statistics(queries, keys, width, scale):
    heads, length, _ = queries.shape
    blocks = length // width

    def row_outer(i, state):
        i = jnp.asarray(i).astype(jnp.int32)
        peak_all, total_all = state
        q_block = lax.dynamic_slice_in_dim(queries, i * width, width, 1)

        def row_inner(j, carry):
            j = jnp.asarray(j).astype(jnp.int32)
            peak, total = carry
            k_block = lax.dynamic_slice_in_dim(keys, j * width, width, 1)
            scores = block_scores(q_block, k_block, i * width, j * width, scale)
            fresh = jnp.maximum(peak, jnp.max(scores, axis=2))
            total = total * jnp.exp(peak - fresh) + jnp.sum(
                jnp.exp(scores - fresh[:, :, None]), axis=2
            )
            return (fresh, total)

        starting = (
            jnp.full((heads, width), big_negative, jnp.float32),
            jnp.zeros((heads, width), jnp.float32),
        )
        peak, total = lax.fori_loop(0, i + 1, row_inner, starting)
        peak_all = lax.dynamic_update_slice_in_dim(peak_all, peak, i * width, 1)
        total_all = lax.dynamic_update_slice_in_dim(total_all, total, i * width, 1)
        return (peak_all, total_all)

    starting = (jnp.zeros((heads, length), jnp.float32), jnp.zeros((heads, length), jnp.float32))
    return lax.fori_loop(0, blocks, row_outer, starting)


def attend(queries, keys, values, peak, total, width, scale):
    heads, length, dim = queries.shape
    blocks = length // width

    def attend_outer(i, output):
        i = jnp.asarray(i).astype(jnp.int32)
        q_block = lax.dynamic_slice_in_dim(queries, i * width, width, 1)
        peak_block = lax.dynamic_slice_in_dim(peak, i * width, width, 1)
        total_block = lax.dynamic_slice_in_dim(total, i * width, width, 1)

        def attend_inner(j, running):
            j = jnp.asarray(j).astype(jnp.int32)
            k_block = lax.dynamic_slice_in_dim(keys, j * width, width, 1)
            v_block = lax.dynamic_slice_in_dim(values, j * width, width, 1)
            scores = block_scores(q_block, k_block, i * width, j * width, scale)
            weights = (jnp.exp(scores - peak_block[:, :, None]) / total_block[:, :, None]).astype(
                jnp.bfloat16
            )
            return running + jnp.einsum(
                "hqk,hkd->hqd", weights, v_block, preferred_element_type=jnp.float32
            )

        running = lax.fori_loop(0, i + 1, attend_inner, jnp.zeros((heads, width, dim), jnp.float32))
        return lax.dynamic_update_slice_in_dim(output, running.astype(jnp.bfloat16), i * width, 1)

    return lax.fori_loop(0, blocks, attend_outer, jnp.zeros((heads, length, dim), jnp.bfloat16))


def value_grads(queries, keys, d_out, peak, total, width, scale):
    heads, length, dim = queries.shape
    blocks = length // width

    def value_outer(j, output):
        j = jnp.asarray(j).astype(jnp.int32)
        k_block = lax.dynamic_slice_in_dim(keys, j * width, width, 1)

        def value_inner(i, running):
            i = jnp.asarray(i).astype(jnp.int32)
            q_block = lax.dynamic_slice_in_dim(queries, i * width, width, 1)
            d_block = lax.dynamic_slice_in_dim(d_out, i * width, width, 1)
            peak_block = lax.dynamic_slice_in_dim(peak, i * width, width, 1)
            total_block = lax.dynamic_slice_in_dim(total, i * width, width, 1)
            scores = block_scores(q_block, k_block, i * width, j * width, scale)
            weights = (jnp.exp(scores - peak_block[:, :, None]) / total_block[:, :, None]).astype(
                jnp.bfloat16
            )
            return running + jnp.einsum(
                "hqk,hqd->hkd", weights, d_block, preferred_element_type=jnp.float32
            )

        running = lax.fori_loop(j, blocks, value_inner, jnp.zeros((heads, width, dim), jnp.float32))
        return lax.dynamic_update_slice_in_dim(output, running.astype(jnp.bfloat16), j * width, 1)

    return lax.fori_loop(0, blocks, value_outer, jnp.zeros((heads, length, dim), jnp.bfloat16))


def local(queries, keys, hidden, value_weight, readout, base_logits, labels, hessian):
    seq_count = lax.axis_size("seq")
    data_count = lax.axis_size("dp")
    token_rows = queries.shape[1]
    heads = queries.shape[2] // HD
    kv_heads = keys.shape[2] // HD
    kv_width = keys.shape[2]
    group = heads // kv_heads
    local_heads = heads // seq_count
    spread_factor = max(1, group // local_heads)
    local_kv = kv_heads * spread_factor // seq_count
    length = token_rows * seq_count
    width = min(512, length)
    scale = 1.0 / math.sqrt(HD)
    columns = lax.all_to_all(hidden, "dp", split_axis=2, concat_axis=0, tiled=True)
    values = sum_at_owner(
        jnp.einsum("std,dk->stk", columns, value_weight, preferred_element_type=jnp.float32).astype(
            jnp.bfloat16
        ),
        "dp",
        0,
    )
    values = values.astype(jnp.bfloat16)

    def widen(array):
        split = array.reshape(1, token_rows, kv_heads, 1, HD)
        split = jnp.broadcast_to(split, (1, token_rows, kv_heads, spread_factor, HD))
        return split.reshape(1, token_rows, seq_count, local_kv * HD)

    paired = jnp.concatenate((widen(keys), widen(values)), axis=3)
    paired = paired.reshape(1, token_rows, seq_count * 2 * local_kv * HD)
    head_queries, head_pairs = (
        several_exchanges(queries, "seq", 2, 2, 1),
        several_exchanges(paired, "seq", 2, 2, 1),
    )

    def heads_first(array, count):
        return array[0].reshape(length, count, HD).transpose(1, 0, 2)

    q_local = heads_first(head_queries, local_heads)
    pair_local = head_pairs[0].reshape(length, 2, local_kv, HD)
    k_local = jnp.repeat(pair_local[:, 0].transpose(1, 0, 2), local_heads // local_kv, axis=0)
    v_local = jnp.repeat(pair_local[:, 1].transpose(1, 0, 2), local_heads // local_kv, axis=0)
    peak, total = row_statistics(q_local, k_local, width, scale)
    attended = attend(q_local, k_local, v_local, peak, total, width, scale)
    attended = attended.transpose(1, 0, 2).reshape(1, length, local_heads * HD)
    mixed = several_exchanges(attended, "seq", 2, 1, 2)
    logits = base_logits[0] + jnp.dot(mixed[0], readout, preferred_element_type=jnp.float32)
    softmax_rows = jax.nn.softmax(logits, axis=1)
    chosen = labels[0][:, None] == lax.broadcasted_iota(jnp.int32, logits.shape, 1)
    d_logits = (softmax_rows - chosen.astype(jnp.float32)).astype(jnp.bfloat16)
    d_mixed = jnp.einsum("tc,ec->te", d_logits, readout, preferred_element_type=jnp.float32).astype(
        jnp.bfloat16
    )
    d_heads = several_exchanges(d_mixed[None], "seq", 2, 2, 1)
    d_local = heads_first(d_heads, local_heads)
    d_head = value_grads(q_local, k_local, d_local, peak, total, width, scale)
    d_head = d_head.transpose(1, 0, 2).reshape(1, length, local_heads * HD)
    d_tokens = lax.all_to_all(d_head, "seq", split_axis=1, concat_axis=2, tiled=True)
    d_values = d_tokens[0].astype(jnp.float32).reshape(token_rows, kv_heads, group, HD).sum(axis=2)
    d_values = d_values.reshape(1, token_rows, kv_width).astype(jnp.bfloat16)
    partial_value = jnp.einsum(
        "stk,std->kd", collect(d_values, "dp", 0), columns, preferred_element_type=jnp.float32
    )
    grad_sum = sum_at_owner(partial_value.astype(jnp.bfloat16), "seq", 0)
    tokens_all = length * data_count
    estimate = grad_sum * grad_sum / tokens_all
    return (estimate, beta_two * hessian + (1.0 - beta_two) * estimate)


def solution(mesh):
    placed = (
        P("dp", "seq", None),
        P("dp", "seq", None),
        P("dp", "seq", None),
        P("dp", None),
        P(),
        P("dp", "seq", None),
        P("dp", "seq"),
        P("seq", "dp"),
    )
    return jax.shard_map(
        local,
        mesh=mesh,
        in_specs=placed,
        out_specs=(P("seq", "dp"), P("seq", "dp")),
        check_vma=False,
    )
```

profile of v0, /device:TPU:8, one launch (start us, length us, event | category | flops | bytes accessed | tf_op | source)
XLA Modules:
  0.0 691.2 jit_solution(15799862219191184211)
XLA Ops:
  0.6 5.7 copy.51
  6.8 23.3 %reduce.11 = bf16[4096,128]{1,0:T(8,128)(2,1)S(1)} reduce(bf16[4096,1,128]{2,1,0:T(2,128)(2,1)} %bitcast.184, bf16[]{:T(256)} %broadcast.149), dimensions={1}, to_apply=%bitcast.130.reduce_sub_computation | reduce | bytes 2097154
  31.3 4.3 all-to-all-start
  39.0 2.4 copy.59
  41.3 10.3 %all-to-all-done = bf16[8,2,32768]{2,1,0:T(2,128)(2,1)} async-done(((bf16[8,2,32768]{2,1,0:T(2,128)(2,1)}), bf16[8,2,32768]{2,1,0:T(2,128)(2,1)}, u32[]{:S(2)}, u32[]{:S(2)}) %all-to-all-start) | async-done | bytes 1048608 | tf_op jit(solution)/shard_map/all_to_all | solution.py:167
  51.6 11.8 %all-to-all-start.4 = ((bf16[32,1,64,128]{3,2,1,0:T(8,128)(2,1)}), bf16[32,1,64,128]{3,2,1,0:T(8,128)(2,1)}, u32[]{:S(2)}, u32[]{:S(2)}) async-start(bf16[32,1,64,128]{3,2,1,0:T(8,128)(2,1)} %copy.59), calls=%async_computation.4 | async-start | bytes 1048576 | tf_op jit(solution)/shard_map/all_to_all | solution.py:42
  63.4 5.8 reshape.162
  72.2 4.1 convert_bitcast_fusion
  76.3 3.6 all-to-all-done.4
  80.0 4.4 all-to-all-start.1
  85.5 26.0 %all-to-all-done.1 = bf16[8,1,128,1024]{3,2,1,0:T(8,128)(2,1)} async-done(((bf16[8,1,128,1024]{3,2,1,0:T(8,128)(2,1)}), bf16[8,1,128,1024]{3,2,1,0:T(8,128)(2,1)}, u32[]{:S(2)}, u32[]{:S(2)}) %all-to-all-start.1) | async-done | bytes 2097184 | tf_op jit(solution)/shard_map/all_to_all | solution.py:19
  111.5 6.3 all-to-all-start.5
  122.1 12.3 %all-to-all-done.5 = bf16[32,1,64,128]{3,2,1,0:T(8,128)(2,1)} async-done(((bf16[32,1,64,128]{3,2,1,0:T(8,128)(2,1)}), bf16[32,1,64,128]{3,2,1,0:T(8,128)(2,1)}, u32[]{:S(2)}, u32[]{:S(2)}) %all-to-all-start.5) | async-done | bytes 524320 | tf_op jit(solution)/shard_map/all_to_all | solution.py:42
  134.4 32.7 %all_to_all.82 = bf16[32,1,64,256]{3,2,1,0:T(8,128)(2,1)} all-to-all(bf16[32,1,64,256]{3,2,1,0:T(8,128)(2,1)S(1)} %get-tuple-element.816), channel_id=1, replica_groups=mesh['seq'=32,'dp'=8] {'seq'}, dimensions={0} | all-to-all | bytes 2097152 | tf_op jit(solution)/shard_map/all_to_all | solution.py:42
  167.1 5.6 all-to-all-start.3
  174.0 25.5 %all-to-all-done.3 = bf16[32,1,64,256]{3,2,1,0:T(8,128)(2,1)} async-done(((bf16[32,1,64,256]{3,2,1,0:T(8,128)(2,1)}), bf16[32,1,64,256]{3,2,1,0:T(8,128)(2,1)}, u32[]{:S(2)}, u32[]{:S(2)}) %all-to-all-start.3) | async-done | bytes 1048608 | tf_op jit(solution)/shard_map/all_to_all | solution.py:42
  199.6 3.1 pad_maximum_fusion
  202.7 4.0 reshape.160
  206.6 6.8 fusion.74
  213.4 5.4 copy.75
  218.9 2.3 copy.69
  222.4 59.3 %while.120 = (s32[]{:T(128)}, f32[1,4096]{1,0:T(1,128)}, f32[1,4096]{1,0:T(1,128)}, bf16[1,4096,128]{2,1,0:T(8,128)(2,1)S(1)}, bf16[1,4096,128]{2,1,0:T(8,128)(2...) while((s32[]{:T(128)}, f32[1,4096]{1,0:T(1,128)}, ...), condition=%wide.region_6.7_spmd, body=%wide.region_1.6_spmd.sunk | while | flops 68683792 | bytes 2669010 | solution.py:94
  224.5 3.0 while.125
  228.2 4.5 while.125
  233.4 6.0 while.125
  240.0 7.5 %while.125 = (s32[]{:T(128)}, f32[1,512]{1,0:T(1,128)S(1)}, f32[1,512]{1,0:T(1,128)S(1)}, s32[]{:T(128)}, s32[]{:T(128)}, /*index=5*/bf16[1,4096,128]{2,1,0:T(8,...) while((s32[]{:T(128)}, f32[1,512]{1,0:T(1,128)S(1)}, ...), condition=%wide.region_5.5_spmd, body=%wide.region_2.4_spmd.sunk | while | flops 68683784 | bytes 2394279 | solution.py:88
  248.2 9.0 %while.125 = (s32[]{:T(128)}, f32[1,512]{1,0:T(1,128)S(1)}, f32[1,512]{1,0:T(1,128)S(1)}, s32[]{:T(128)}, s32[]{:T(128)}, /*index=5*/bf16[1,4096,128]{2,1,0:T(8,...) while((s32[]{:T(128)}, f32[1,512]{1,0:T(1,128)S(1)}, ...), condition=%wide.region_5.5_spmd, body=%wide.region_2.4_spmd.sunk | while | flops 68683784 | bytes 2394279 | solution.py:88
  257.9 10.5 %while.125 = (s32[]{:T(128)}, f32[1,512]{1,0:T(1,128)S(1)}, f32[1,512]{1,0:T(1,128)S(1)}, s32[]{:T(128)}, s32[]{:T(128)}, /*index=5*/bf16[1,4096,128]{2,1,0:T(8,...) while((s32[]{:T(128)}, f32[1,512]{1,0:T(1,128)S(1)}, ...), condition=%wide.region_5.5_spmd, body=%wide.region_2.4_spmd.sunk | while | flops 68683784 | bytes 2394279 | solution.py:88
  269.0 12.1 %while.125 = (s32[]{:T(128)}, f32[1,512]{1,0:T(1,128)S(1)}, f32[1,512]{1,0:T(1,128)S(1)}, s32[]{:T(128)}, s32[]{:T(128)}, /*index=5*/bf16[1,4096,128]{2,1,0:T(8,...) while((s32[]{:T(128)}, f32[1,512]{1,0:T(1,128)S(1)}, ...), condition=%wide.region_5.5_spmd, body=%wide.region_2.4_spmd.sunk | while | flops 68683784 | bytes 2394279 | solution.py:88
  281.7 5.4 copy.76
  287.1 2.3 copy.63
  290.5 74.3 %while.122 = (s32[]{:T(128)}, bf16[1,4096,128]{2,1,0:T(8,128)(2,1)}, bf16[1,4096,128]{2,1,0:T(8,128)(2,1)S(1)}, f32[1,4096]{1,0:T(1,128)}, f32[1,4096]{1,0:T(1,1...) while((s32[]{:T(128)}, bf16[1,4096,128]{2,1,0:T(8,128)(2,1)}, ...), condition=%wide.region_10.11_spmd, body=%wide.region_7.10_spmd.sunk | while | flops 135922688 | bytes 1857014 | solution.py:122
  294.4 3.5 while.126
  299.4 5.2 while.126
  306.0 7.0 %while.126 = (s32[]{:T(128)}, f32[1,512,128]{2,1,0:T(8,128)S(1)}, s32[]{:T(128)}, s32[]{:T(128)}, bf16[1,4096,128]{2,1,0:T(8,128)(2,1)}, /*index=5*/bf16[1,512,1...) while((s32[]{:T(128)}, f32[1,512,128]{2,1,0:T(8,128)S(1)}, ...), condition=%wide.region_9.9_spmd, body=%wide.region_8.8_spmd.sunk | while | flops 135857152 | bytes 930995 | solution.py:119
  314.4 8.7 %while.126 = (s32[]{:T(128)}, f32[1,512,128]{2,1,0:T(8,128)S(1)}, s32[]{:T(128)}, s32[]{:T(128)}, bf16[1,4096,128]{2,1,0:T(8,128)(2,1)}, /*index=5*/bf16[1,512,1...) while((s32[]{:T(128)}, f32[1,512,128]{2,1,0:T(8,128)S(1)}, ...), condition=%wide.region_9.9_spmd, body=%wide.region_8.8_spmd.sunk | while | flops 135857152 | bytes 930995 | solution.py:119
  324.6 10.5 %while.126 = (s32[]{:T(128)}, f32[1,512,128]{2,1,0:T(8,128)S(1)}, s32[]{:T(128)}, s32[]{:T(128)}, bf16[1,4096,128]{2,1,0:T(8,128)(2,1)}, /*index=5*/bf16[1,512,1...) while((s32[]{:T(128)}, f32[1,512,128]{2,1,0:T(8,128)S(1)}, ...), condition=%wide.region_9.9_spmd, body=%wide.region_8.8_spmd.sunk | while | flops 135857152 | bytes 930995 | solution.py:119
  336.5 12.2 %while.126 = (s32[]{:T(128)}, f32[1,512,128]{2,1,0:T(8,128)S(1)}, s32[]{:T(128)}, s32[]{:T(128)}, bf16[1,4096,128]{2,1,0:T(8,128)(2,1)}, /*index=5*/bf16[1,512,1...) while((s32[]{:T(128)}, f32[1,512,128]{2,1,0:T(8,128)S(1)}, ...), condition=%wide.region_9.9_spmd, body=%wide.region_8.8_spmd.sunk | while | flops 135857152 | bytes 930995 | solution.py:119
  350.2 14.0 %while.126 = (s32[]{:T(128)}, f32[1,512,128]{2,1,0:T(8,128)S(1)}, s32[]{:T(128)}, s32[]{:T(128)}, bf16[1,4096,128]{2,1,0:T(8,128)(2,1)}, /*index=5*/bf16[1,512,1...) while((s32[]{:T(128)}, f32[1,512,128]{2,1,0:T(8,128)S(1)}, ...), condition=%wide.region_9.9_spmd, body=%wide.region_8.8_spmd.sunk | while | flops 135857152 | bytes 930995 | solution.py:119
  366.9 20.7 %all_to_all.83 = bf16[32,1,64,128]{3,2,1,0:T(8,128)(2,1)} all-to-all(bf16[32,1,64,128]{3,2,1,0:T(8,128)(2,1)S(1)} %get-tuple-element.820), channel_id=1, replica_groups=mesh['seq'=32,'dp'=8] {'seq'}, dimensions={0} | all-to-all | bytes 1048576 | tf_op jit(solution)/shard_map/all_to_all | solution.py:42
  387.6 5.6 all-to-all-start.7
  393.2 2.4 copy.66
  395.6 12.8 %all-to-all-done.7 = bf16[32,1,64,128]{3,2,1,0:T(8,128)(2,1)} async-done(((bf16[32,1,64,128]{3,2,1,0:T(8,128)(2,1)}), bf16[32,1,64,128]{3,2,1,0:T(8,128)(2,1)}, u32[]{:S(2)}, u32[]{:S(2)}) %all-to-all-start.7) | async-done | bytes 524320 | tf_op jit(solution)/shard_map/all_to_all | solution.py:42
  408.5 2.4 copy.67
  410.9 2.1 pad_maximum_fusion.2
  416.2 20.2 %all_to_all.84 = bf16[32,1,64,128]{3,2,1,0:T(8,128)(2,1)} all-to-all(bf16[32,1,64,128]{3,2,1,0:T(8,128)(2,1)S(1)} %get-tuple-element.818), channel_id=1, replica_groups=mesh['seq'=32,'dp'=8] {'seq'}, dimensions={0} | all-to-all | bytes 1048576 | tf_op jit(solution)/shard_map/all_to_all | solution.py:42
  436.4 5.6 all-to-all-start.9
  442.1 14.2 %all-to-all-done.9 = bf16[32,1,64,128]{3,2,1,0:T(8,128)(2,1)} async-done(((bf16[32,1,64,128]{3,2,1,0:T(8,128)(2,1)}), bf16[32,1,64,128]{3,2,1,0:T(8,128)(2,1)}, u32[]{:S(2)}, u32[]{:S(2)}) %all-to-all-start.9) | async-done | bytes 524320 | tf_op jit(solution)/shard_map/all_to_all | solution.py:42
  456.3 2.3 pad_maximum_fusion.3
  459.7 99.4 %while.124 = (s32[]{:T(128)}, bf16[1,4096,128]{2,1,0:T(8,128)(2,1)}, bf16[1,4096,128]{2,1,0:T(8,128)(2,1)}, bf16[1,4096,128]{2,1,0:T(8,128)(2,1)S(1)}, f32[1,409...) while((s32[]{:T(128)}, bf16[1,4096,128]{2,1,0:T(8,128)(2,1)}, ...), condition=%wide.region_16.17_spmd, body=%wide.region_13.16_spmd.sunk | while | flops 135922688 | bytes 1856998 | solution.py:150
  460.6 19.2 %while.127 = (s32[]{:T(128)}, f32[1,512,128]{2,1,0:T(8,128)S(1)}, s32[]{:T(128)}, bf16[1,4096,128]{2,1,0:T(8,128)(2,1)S(1)}, bf16[1,512,128]{2,1,0:T(8,128)(2,1)...) while((s32[]{:T(128)}, f32[1,512,128]{2,1,0:T(8,128)S(1)}, ...), condition=%wide.region_15.15_spmd, body=%wide.region_14.14_spmd.sunk | while | flops 135857152 | bytes 939183 | solution.py:147
  481.4 16.8 %while.127 = (s32[]{:T(128)}, f32[1,512,128]{2,1,0:T(8,128)S(1)}, s32[]{:T(128)}, bf16[1,4096,128]{2,1,0:T(8,128)(2,1)S(1)}, bf16[1,512,128]{2,1,0:T(8,128)(2,1)...) while((s32[]{:T(128)}, f32[1,512,128]{2,1,0:T(8,128)S(1)}, ...), condition=%wide.region_15.15_spmd, body=%wide.region_14.14_spmd.sunk | while | flops 135857152 | bytes 939183 | solution.py:147
  499.9 14.4 %while.127 = (s32[]{:T(128)}, f32[1,512,128]{2,1,0:T(8,128)S(1)}, s32[]{:T(128)}, bf16[1,4096,128]{2,1,0:T(8,128)(2,1)S(1)}, bf16[1,512,128]{2,1,0:T(8,128)(2,1)...) while((s32[]{:T(128)}, f32[1,512,128]{2,1,0:T(8,128)S(1)}, ...), condition=%wide.region_15.15_spmd, body=%wide.region_14.14_spmd.sunk | while | flops 135857152 | bytes 939183 | solution.py:147
  515.9 12.0 %while.127 = (s32[]{:T(128)}, f32[1,512,128]{2,1,0:T(8,128)S(1)}, s32[]{:T(128)}, bf16[1,4096,128]{2,1,0:T(8,128)(2,1)S(1)}, bf16[1,512,128]{2,1,0:T(8,128)(2,1)...) while((s32[]{:T(128)}, f32[1,512,128]{2,1,0:T(8,128)S(1)}, ...), condition=%wide.region_15.15_spmd, body=%wide.region_14.14_spmd.sunk | while | flops 135857152 | bytes 939183 | solution.py:147
  529.5 9.6 %while.127 = (s32[]{:T(128)}, f32[1,512,128]{2,1,0:T(8,128)S(1)}, s32[]{:T(128)}, bf16[1,4096,128]{2,1,0:T(8,128)(2,1)S(1)}, bf16[1,512,128]{2,1,0:T(8,128)(2,1)...) while((s32[]{:T(128)}, f32[1,512,128]{2,1,0:T(8,128)S(1)}, ...), condition=%wide.region_15.15_spmd, body=%wide.region_14.14_spmd.sunk | while | flops 135857152 | bytes 939183 | solution.py:147
  540.7 7.2 %while.127 = (s32[]{:T(128)}, f32[1,512,128]{2,1,0:T(8,128)S(1)}, s32[]{:T(128)}, bf16[1,4096,128]{2,1,0:T(8,128)(2,1)S(1)}, bf16[1,512,128]{2,1,0:T(8,128)(2,1)...) while((s32[]{:T(128)}, f32[1,512,128]{2,1,0:T(8,128)S(1)}, ...), condition=%wide.region_15.15_spmd, body=%wide.region_14.14_spmd.sunk | while | flops 135857152 | bytes 939183 | solution.py:147
  549.6 4.8 while.127
  556.0 2.4 while.127
  559.1 4.3 copy.82
  563.4 23.3 %reduce.12 = bf16[4096,128]{1,0:T(8,128)(2,1)S(1)} reduce(bf16[4096,1,128]{2,1,0:T(2,128)(2,1)} %bitcast.185, bf16[]{:T(256)} %broadcast.149), dimensions={1}, to_apply=%bitcast.143.reduce_sub_computation | reduce | bytes 2097154
  587.8 30.6 %all_to_all.87 = bf16[32,2,8192]{2,1,0:T(2,128)(2,1)S(1)} all-to-all(bf16[32,2,8192]{2,1,0:T(2,128)(2,1)} %reshape.163), channel_id=1, replica_groups=mesh['seq'=32,'dp'=8] {'seq'}, dimensions={0} | all-to-all | bytes 2097152 | tf_op jit(solution)/shard_map/all_to_all | solution.py:211
  618.5 3.5 reshape.164
  624.4 31.5 %all_to_all.85 = bf16[8,1,128,1024]{2,3,1,0:T(8,128)(2,1)S(1)} all-to-all(bf16[8,1,128,1024]{2,3,1,0:T(8,128)(2,1)S(1)} %broadcast_in_dim.44), channel_id=1, replica_groups=mesh['seq'=32,'dp'=8] {'dp'}, dimensions={0} | all-to-all | bytes 4194304 | tf_op jit(solution)/shard_map/all_to_all | solution.py:48
  657.1 33.2 %all_to_all.86 = bf16[32,32,512]{2,1,0:T(8,128)(2,1)S(1)} all-to-all(bf16[32,32,512]{2,1,0:T(8,128)(2,1)S(1)} %bitcast.203), channel_id=1, replica_groups=mesh['seq'=32,'dp'=8] {'seq'}, dimensions={0} | all-to-all | bytes 2097152 | tf_op jit(solution)/shard_map/all_to_all | solution.py:19
  (536 shorter events, 260.3 us)
Async XLA Ops:
  0.6 412.4 %copy-start = (bf16[4096,256]{1,0:T(8,128)(2,1)S(1)}, bf16[4096,256]{1,0:T(8,128)(2,1)}, u32[]{:S(2)}) copy-start(bf16[4096,256]{1,0:T(8,128)(2,1)} %param.24) | copy-start | bytes 6291460
  31.3 20.3 %all-to-all-start = ((bf16[8,2,32768]{2,1,0:T(2,128)(2,1)}), bf16[8,2,32768]{2,1,0:T(2,128)(2,1)}, u32[]{:S(2)}, u32[]{:S(2)}) async-start(bf16[8,2,32768]{2,1,0:T(2,128)(2,1)} %reshape.161), calls=%async_computation | async-start | bytes 2097152 | tf_op jit(solution)/shard_map/all_to_all | solution.py:167
  51.6 28.3 %all-to-all-start.4 = ((bf16[32,1,64,128]{3,2,1,0:T(8,128)(2,1)}), bf16[32,1,64,128]{3,2,1,0:T(8,128)(2,1)}, u32[]{:S(2)}, u32[]{:S(2)}) async-start(bf16[32,1,64,128]{3,2,1,0:T(8,128)(2,1)} %copy.59), calls=%async_computation.4 | async-start | bytes 1048576 | tf_op jit(solution)/shard_map/all_to_all | solution.py:42
  76.3 8.0 %copy-start.1 = (bf16[32,1,64,128]{2,3,0,1:T(8,128)(2,1)S(1)}, bf16[32,1,64,128]{2,3,0,1:T(8,128)(2,1)}, u32[]{:S(2)}) copy-start(bf16[32,1,64,128]{2,3,0,1:T(8,128)(2,1)} %get-tuple-element.823) | copy-start | bytes 1572868
  80.0 31.5 %all-to-all-start.1 = ((bf16[8,1,128,1024]{3,2,1,0:T(8,128)(2,1)}), bf16[8,1,128,1024]{3,2,1,0:T(8,128)(2,1)}, u32[]{:S(2)}, u32[]{:S(2)}) async-start(bf16[8,1,128,1024]{3,2,1,0:T(8,128)(2,1)} %convert_bitcast_fusion), calls=%async_computation.1 | async-start | bytes 4194304 | tf_op jit(solution)/shard_map/all_to_all | solution.py:19
  84.3 33.5 %copy-start.3 = (bf16[1,128,1024]{2,1,0:T(8,128)(2,1)S(1)}, bf16[1,128,1024]{2,1,0:T(8,128)(2,1)}, u32[]{:S(2)}) copy-start(bf16[1,128,1024]{2,1,0:T(8,128)(2,1)} %param.21) | copy-start | bytes 786436
  111.5 22.9 %all-to-all-start.5 = ((bf16[32,1,64,128]{3,2,1,0:T(8,128)(2,1)}), bf16[32,1,64,128]{3,2,1,0:T(8,128)(2,1)}, u32[]{:S(2)}, u32[]{:S(2)}) async-start(bf16[32,1,64,128]{3,2,1,0:T(8,128)(2,1)} %copy.60), calls=%async_computation.5 | async-start | bytes 1048576 | tf_op jit(solution)/shard_map/all_to_all | solution.py:42
  167.1 32.5 %all-to-all-start.3 = ((bf16[32,1,64,256]{3,2,1,0:T(8,128)(2,1)}), bf16[32,1,64,256]{3,2,1,0:T(8,128)(2,1)}, u32[]{:S(2)}, u32[]{:S(2)}) async-start(bf16[32,1,64,256]{3,2,1,0:T(8,128)(2,1)} %get-tuple-element.817), calls=%async_computation.3 | async-start | bytes 2097152 | tf_op jit(solution)/shard_map/all_to_all | solution.py:42
  387.6 20.8 %all-to-all-start.7 = ((bf16[32,1,64,128]{3,2,1,0:T(8,128)(2,1)}), bf16[32,1,64,128]{3,2,1,0:T(8,128)(2,1)}, u32[]{:S(2)}, u32[]{:S(2)}) async-start(bf16[32,1,64,128]{3,2,1,0:T(8,128)(2,1)} %get-tuple-element.821), calls=%async_computation.7 | async-start | bytes 1048576 | tf_op jit(solution)/shard_map/all_to_all | solution.py:42
  395.6 17.4 %copy-start.4 = (f32[1,128,256]{2,1,0:T(8,128)S(1)}, f32[1,128,256]{2,1,0:T(8,128)}, u32[]{:S(2)}) copy-start(f32[1,128,256]{2,1,0:T(8,128)} %param.25) | copy-start | bytes 393220
  413.0 0.8 copy-start.6
  436.4 19.8 %all-to-all-start.9 = ((bf16[32,1,64,128]{3,2,1,0:T(8,128)(2,1)}), bf16[32,1,64,128]{3,2,1,0:T(8,128)(2,1)}, u32[]{:S(2)}, u32[]{:S(2)}) async-start(bf16[32,1,64,128]{3,2,1,0:T(8,128)(2,1)} %get-tuple-element.819), calls=%async_computation.9 | async-start | bytes 1048576 | tf_op jit(solution)/shard_map/all_to_all | solution.py:42
  624.3 31.5 %copy-start.2 = (bf16[1,128,8,512]{3,1,2,0:T(8,128)(2,1)S(1)}, bf16[1,128,8,512]{3,1,2,0:T(8,128)(2,1)}, u32[]{:S(2)}) copy-start(bf16[1,128,8,512]{3,1,2,0:T(8,128)(2,1)} %copy.52) | copy-start | bytes 3145732
  657.1 33.4 %copy-start.5 = (f32[32,512]{1,0:T(8,128)S(1)}, f32[32,512]{1,0:T(8,128)}, u32[]{:S(2)}) copy-start(f32[32,512]{1,0:T(8,128)} %param.27) | copy-start | bytes 196612
where the time goes:
time: 697 us; the launch traced here: 691 us
  matrix products  172 us (25%)
  blocking collectives  169 us (24%)
  local copies, waits for them, and re-layouts  118 us (17%)
  waiting for transfers between devices  105 us (15%)
  other arithmetic  78 us (11%)
  starting transfers between devices  43.6 us (6%)
    all_to_all x3, blocking collectives, several_exchanges(): lax.all_to_all(share, axis, split_axis=0, concat_axis=0, tiled=True)  73.6 us
    all_to_all x5, waiting for transfers between devices, several_exchanges(): lax.all_to_all(share, axis, split_axis=0, concat_axis=0, tiled=True)  68.5 us
    dot_general x36, matrix products, attend_inner(): jnp.einsum('hqk,hkd->hqd', weights, v_block, preferred_element_type=jnp.f...  61.3 us
    dot_general x36, matrix products, value_inner(): jnp.einsum('hqk,hqd->hkd', weights, d_block, preferred_element_type=jnp.f...  59.8 us
    unnamed x2, other arithmetic  46.7 us
    dot_general x36, matrix products, block_scores(): jnp.einsum('hqd,hkd->hqk', q_block, k_block, preferred_element_type=jnp.f...  44.3 us
    all_to_all x5, starting transfers between devices, several_exchanges(): lax.all_to_all(share, axis, split_axis=0, concat_axis=0, tiled=True)  35 us
    unnamed x27, local copies, waits for them, and re-layouts  33.9 us
  transfers between devices with their start and end apart: 7, of which 7 were waited for; matrix products, arithmetic and copies ran while one was open for 4% of the time, Pallas kernels for 0%

commit v1 on v0

--- a/solution.py
+++ b/solution.py
@@ -7,6 +7,12 @@
 HD = 128
 big_negative = -1e30
 beta_two = 0.99
+
+
+def exchange_blocks(array, axis, split, join):
+    pieces = jnp.split(array, lax.axis_size(axis), axis=split)
+    incoming = lax.all_to_all(jnp.stack(pieces), axis, 0, 0)
+    return jnp.concatenate(incoming, axis=join)
 
 
 def in_blocks(x, dim, count):
@@ -164,7 +170,7 @@
     length = token_rows * seq_count
     width = min(512, length)
     scale = 1.0 / math.sqrt(HD)
-    columns = lax.all_to_all(hidden, "dp", split_axis=2, concat_axis=0, tiled=True)
+    columns = exchange_blocks(hidden, "dp", 2, 0)
     values = sum_at_owner(
         jnp.einsum("std,dk->stk", columns, value_weight, preferred_element_type=jnp.float32).astype(
             jnp.bfloat16

time: 697 us -> 678 us (0.973)
  other arithmetic: 78 us -> 54.7 us
  waiting for transfers between devices: 105 us -> 114 us
    unnamed x2 -> x1, other arithmetic: 46.7 us -> 23.4 us
    all_to_all x5, waiting for transfers between devices: 68.5 us -> 77.7 us  [several_exchanges(): lax.all_to_all(share, axis, split_axis=0, concat_axis=0, tiled=True)]
    unnamed x27 -> x30, local copies, waits for them, and re-layouts: 33.9 us -> 30.6 us
  transfers between devices with their start and end apart: 7 -> 7, of which waited for: 7 -> 7; matrix products, arithmetic and copies ran while one was open for 4% -> 3% of each run, Pallas kernels for 0% -> 0%
where the time goes in v1:
time: 678 us; the launch traced here: 672 us
  matrix products  173 us (26%)
  blocking collectives  167 us (25%)
  local copies, waits for them, and re-layouts  115 us (17%)
  waiting for transfers between devices  114 us (17%)
  other arithmetic  54.7 us (8%)
  starting transfers between devices  42.9 us (6%)
    all_to_all x5, waiting for transfers between devices, several_exchanges(): lax.all_to_all(share, axis, split_axis=0, concat_axis=0, tiled=True)  77.7 us
    all_to_all x3, blocking collectives, several_exchanges(): lax.all_to_all(share, axis, split_axis=0, concat_axis=0, tiled=True)  73.5 us
    dot_general x36, matrix products, attend_inner(): jnp.einsum('hqk,hkd->hqd', weights, v_block, preferred_element_type=jnp.f...  61.2 us
    dot_general x36, matrix products, value_inner(): jnp.einsum('hqk,hqd->hkd', weights, d_block, preferred_element_type=jnp.f...  59.8 us
    dot_general x36, matrix products, block_scores(): jnp.einsum('hqd,hkd->hqk', q_block, k_block, preferred_element_type=jnp.f...  44.3 us
    all_to_all x5, starting transfers between devices, several_exchanges(): lax.all_to_all(share, axis, split_axis=0, concat_axis=0, tiled=True)  34.3 us
    all_to_all x1, blocking collectives, sum_at_owner(): lax.all_to_all(blocks, axis, split_axis=0, concat_axis=0, tiled=True)  33.2 us
    all_to_all x1, blocking collectives, local(): lax.all_to_all(d_head, 'seq', split_axis=1, concat_axis=2, tiled=True)  30.6 us
  transfers between devices with their start and end apart: 7, of which 7 were waited for; matrix products, arithmetic and copies ran while one was open for 3% of the time, Pallas kernels for 0%

profile of v1, /device:TPU:8, one launch (start us, length us, event | category | flops | bytes accessed | tf_op | source)
XLA Modules:
  0.0 672.2 jit_solution(14405800452354773221)
XLA Ops:
  13.3 4.3 all-to-all-start
  21.0 2.5 copy.51
  23.4 10.2 %all-to-all-done = bf16[8,1,128,512]{3,2,1,0:T(8,128)(2,1)} async-done(((bf16[8,1,128,512]{3,2,1,0:T(8,128)(2,1)}), bf16[8,1,128,512]{3,2,1,0:T(8,128)(2,1)}, u32[]{:S(2)}, u32[]{:S(2)}) %all-to-all-start) | async-done | bytes 1048608 | tf_op jit(solution)/shard_map/all_to_all | solution.py:14
  33.6 11.8 %all-to-all-start.4 = ((bf16[32,1,64,128]{3,2,1,0:T(8,128)(2,1)}), bf16[32,1,64,128]{3,2,1,0:T(8,128)(2,1)}, u32[]{:S(2)}, u32[]{:S(2)}) async-start(bf16[32,1,64,128]{3,2,1,0:T(8,128)(2,1)} %copy.51), calls=%async_computation.4 | async-start | bytes 1048576 | tf_op jit(solution)/shard_map/all_to_all | solution.py:48
  45.4 3.8 convert_bitcast_fusion
  49.2 12.8 %all-to-all-done.4 = bf16[32,1,64,128]{3,2,1,0:T(8,128)(2,1)} async-done(((bf16[32,1,64,128]{3,2,1,0:T(8,128)(2,1)}), bf16[32,1,64,128]{3,2,1,0:T(8,128)(2,1)}, u32[]{:S(2)}, u32[]{:S(2)}) %all-to-all-start.4) | async-done | bytes 524320 | tf_op jit(solution)/shard_map/all_to_all | solution.py:48
  62.0 4.3 all-to-all-start.1
  67.5 26.0 %all-to-all-done.1 = bf16[8,1,128,1024]{3,2,1,0:T(8,128)(2,1)} async-done(((bf16[8,1,128,1024]{3,2,1,0:T(8,128)(2,1)}), bf16[8,1,128,1024]{3,2,1,0:T(8,128)(2,1)}, u32[]{:S(2)}, u32[]{:S(2)}) %all-to-all-start.1) | async-done | bytes 2097184 | tf_op jit(solution)/shard_map/all_to_all | solution.py:25
  93.5 5.6 all-to-all-start.5
  99.2 1.9 bitcast_reduce_fusion
  103.4 12.4 %all-to-all-done.5 = bf16[32,1,64,128]{3,2,1,0:T(8,128)(2,1)} async-done(((bf16[32,1,64,128]{3,2,1,0:T(8,128)(2,1)}), bf16[32,1,64,128]{3,2,1,0:T(8,128)(2,1)}, u32[]{:S(2)}, u32[]{:S(2)}) %all-to-all-start.5) | async-done | bytes 524320 | tf_op jit(solution)/shard_map/all_to_all | solution.py:48
  115.8 32.6 %all_to_all.69 = bf16[32,1,64,256]{3,2,1,0:T(8,128)(2,1)} all-to-all(bf16[32,1,64,256]{3,2,1,0:T(8,128)(2,1)S(1)} %get-tuple-element.816), channel_id=1, replica_groups=mesh['seq'=32,'dp'=8] {'seq'}, dimensions={0} | all-to-all | bytes 2097152 | tf_op jit(solution)/shard_map/all_to_all | solution.py:48
  148.4 5.6 all-to-all-start.3
  155.3 25.5 %all-to-all-done.3 = bf16[32,1,64,256]{3,2,1,0:T(8,128)(2,1)} async-done(((bf16[32,1,64,256]{3,2,1,0:T(8,128)(2,1)}), bf16[32,1,64,256]{3,2,1,0:T(8,128)(2,1)}, u32[]{:S(2)}, u32[]{:S(2)}) %all-to-all-start.3) | async-done | bytes 1048608 | tf_op jit(solution)/shard_map/all_to_all | solution.py:48
  180.8 3.1 pad_maximum_fusion
  183.9 4.0 reshape.164
  187.9 6.8 %fusion.74 = (bf16[4096,1,1,128]{3,1,0,2:T(2,128)(2,1)}, bf16[4096,1,1,128]{3,1,0,2:T(2,128)(2,1)}) fusion(bf16[4096,2,1,128]{3,1,0,2:T(2,128)(2,1)} %reshape.164), kind=kLoop, calls=%fused_computation.113 | loop fusion | bytes 4194304 | tf_op jit(solution)/shard_map/slice | solution.py:201
  194.7 5.4 copy.66
  200.1 2.3 copy.61
  203.6 59.3 %while.120 = (s32[]{:T(128)}, f32[1,4096]{1,0:T(1,128)}, f32[1,4096]{1,0:T(1,128)}, bf16[1,4096,128]{2,1,0:T(8,128)(2,1)S(1)}, bf16[1,4096,128]{2,1,0:T(8,128)(2...) while((s32[]{:T(128)}, f32[1,4096]{1,0:T(1,128)}, ...), condition=%wide.region_6.7_spmd, body=%wide.region_1.6_spmd.sunk | while | flops 68683792 | bytes 2669010 | solution.py:100
  205.8 3.0 while.125
  209.5 4.5 while.125
  214.6 6.0 while.125
  221.3 7.5 %while.125 = (s32[]{:T(128)}, f32[1,512]{1,0:T(1,128)S(1)}, f32[1,512]{1,0:T(1,128)S(1)}, s32[]{:T(128)}, s32[]{:T(128)}, /*index=5*/bf16[1,4096,128]{2,1,0:T(8,...) while((s32[]{:T(128)}, f32[1,512]{1,0:T(1,128)S(1)}, ...), condition=%wide.region_5.5_spmd, body=%wide.region_2.4_spmd.sunk | while | flops 68683784 | bytes 2394279 | solution.py:94
  229.5 9.0 %while.125 = (s32[]{:T(128)}, f32[1,512]{1,0:T(1,128)S(1)}, f32[1,512]{1,0:T(1,128)S(1)}, s32[]{:T(128)}, s32[]{:T(128)}, /*index=5*/bf16[1,4096,128]{2,1,0:T(8,...) while((s32[]{:T(128)}, f32[1,512]{1,0:T(1,128)S(1)}, ...), condition=%wide.region_5.5_spmd, body=%wide.region_2.4_spmd.sunk | while | flops 68683784 | bytes 2394279 | solution.py:94
  239.1 10.5 %while.125 = (s32[]{:T(128)}, f32[1,512]{1,0:T(1,128)S(1)}, f32[1,512]{1,0:T(1,128)S(1)}, s32[]{:T(128)}, s32[]{:T(128)}, /*index=5*/bf16[1,4096,128]{2,1,0:T(8,...) while((s32[]{:T(128)}, f32[1,512]{1,0:T(1,128)S(1)}, ...), condition=%wide.region_5.5_spmd, body=%wide.region_2.4_spmd.sunk | while | flops 68683784 | bytes 2394279 | solution.py:94
  250.3 12.1 %while.125 = (s32[]{:T(128)}, f32[1,512]{1,0:T(1,128)S(1)}, f32[1,512]{1,0:T(1,128)S(1)}, s32[]{:T(128)}, s32[]{:T(128)}, /*index=5*/bf16[1,4096,128]{2,1,0:T(8,...) while((s32[]{:T(128)}, f32[1,512]{1,0:T(1,128)S(1)}, ...), condition=%wide.region_5.5_spmd, body=%wide.region_2.4_spmd.sunk | while | flops 68683784 | bytes 2394279 | solution.py:94
  263.0 5.4 copy.67
  268.4 2.3 copy.55
  271.8 74.2 %while.122 = (s32[]{:T(128)}, bf16[1,4096,128]{2,1,0:T(8,128)(2,1)}, bf16[1,4096,128]{2,1,0:T(8,128)(2,1)S(1)}, f32[1,4096]{1,0:T(1,128)}, f32[1,4096]{1,0:T(1,1...) while((s32[]{:T(128)}, bf16[1,4096,128]{2,1,0:T(8,128)(2,1)}, ...), condition=%wide.region_10.11_spmd, body=%wide.region_7.10_spmd.sunk | while | flops 135922688 | bytes 1857014 | solution.py:128
  275.7 3.5 while.126
  280.6 5.2 while.126
  287.3 7.0 %while.126 = (s32[]{:T(128)}, f32[1,512,128]{2,1,0:T(8,128)S(1)}, s32[]{:T(128)}, s32[]{:T(128)}, bf16[1,4096,128]{2,1,0:T(8,128)(2,1)}, /*index=5*/bf16[1,512,1...) while((s32[]{:T(128)}, f32[1,512,128]{2,1,0:T(8,128)S(1)}, ...), condition=%wide.region_9.9_spmd, body=%wide.region_8.8_spmd.sunk | while | flops 135857152 | bytes 930995 | solution.py:125
  295.7 8.7 %while.126 = (s32[]{:T(128)}, f32[1,512,128]{2,1,0:T(8,128)S(1)}, s32[]{:T(128)}, s32[]{:T(128)}, bf16[1,4096,128]{2,1,0:T(8,128)(2,1)}, /*index=5*/bf16[1,512,1...) while((s32[]{:T(128)}, f32[1,512,128]{2,1,0:T(8,128)S(1)}, ...), condition=%wide.region_9.9_spmd, body=%wide.region_8.8_spmd.sunk | while | flops 135857152 | bytes 930995 | solution.py:125
  305.8 10.5 %while.126 = (s32[]{:T(128)}, f32[1,512,128]{2,1,0:T(8,128)S(1)}, s32[]{:T(128)}, s32[]{:T(128)}, bf16[1,4096,128]{2,1,0:T(8,128)(2,1)}, /*index=5*/bf16[1,512,1...) while((s32[]{:T(128)}, f32[1,512,128]{2,1,0:T(8,128)S(1)}, ...), condition=%wide.region_9.9_spmd, body=%wide.region_8.8_spmd.sunk | while | flops 135857152 | bytes 930995 | solution.py:125
  317.7 12.2 %while.126 = (s32[]{:T(128)}, f32[1,512,128]{2,1,0:T(8,128)S(1)}, s32[]{:T(128)}, s32[]{:T(128)}, bf16[1,4096,128]{2,1,0:T(8,128)(2,1)}, /*index=5*/bf16[1,512,1...) while((s32[]{:T(128)}, f32[1,512,128]{2,1,0:T(8,128)S(1)}, ...), condition=%wide.region_9.9_spmd, body=%wide.region_8.8_spmd.sunk | while | flops 135857152 | bytes 930995 | solution.py:125
  331.3 14.0 %while.126 = (s32[]{:T(128)}, f32[1,512,128]{2,1,0:T(8,128)S(1)}, s32[]{:T(128)}, s32[]{:T(128)}, bf16[1,4096,128]{2,1,0:T(8,128)(2,1)}, /*index=5*/bf16[1,512,1...) while((s32[]{:T(128)}, f32[1,512,128]{2,1,0:T(8,128)S(1)}, ...), condition=%wide.region_9.9_spmd, body=%wide.region_8.8_spmd.sunk | while | flops 135857152 | bytes 930995 | solution.py:125
  346.0 2.1 slice_bitcast_fusion.1
  348.0 20.7 %all_to_all.70 = bf16[32,1,64,128]{3,2,1,0:T(8,128)(2,1)} all-to-all(bf16[32,1,64,128]{3,2,1,0:T(8,128)(2,1)S(1)} %get-tuple-element.820), channel_id=1, replica_groups=mesh['seq'=32,'dp'=8] {'seq'}, dimensions={0} | all-to-all | bytes 1048576 | tf_op jit(solution)/shard_map/all_to_all | solution.py:48
  368.7 5.6 all-to-all-start.7
  374.4 2.4 copy.58
  376.8 12.8 %all-to-all-done.7 = bf16[32,1,64,128]{3,2,1,0:T(8,128)(2,1)} async-done(((bf16[32,1,64,128]{3,2,1,0:T(8,128)(2,1)}), bf16[32,1,64,128]{3,2,1,0:T(8,128)(2,1)}, u32[]{:S(2)}, u32[]{:S(2)}) %all-to-all-start.7) | async-done | bytes 524320 | tf_op jit(solution)/shard_map/all_to_all | solution.py:48
  389.6 2.4 copy.59
  392.0 2.1 pad_maximum_fusion.2
  397.3 20.2 %all_to_all.71 = bf16[32,1,64,128]{3,2,1,0:T(8,128)(2,1)} all-to-all(bf16[32,1,64,128]{3,2,1,0:T(8,128)(2,1)S(1)} %get-tuple-element.818), channel_id=1, replica_groups=mesh['seq'=32,'dp'=8] {'seq'}, dimensions={0} | all-to-all | bytes 1048576 | tf_op jit(solution)/shard_map/all_to_all | solution.py:48
  417.5 5.6 all-to-all-start.9
  423.2 14.2 %all-to-all-done.9 = bf16[32,1,64,128]{3,2,1,0:T(8,128)(2,1)} async-done(((bf16[32,1,64,128]{3,2,1,0:T(8,128)(2,1)}), bf16[32,1,64,128]{3,2,1,0:T(8,128)(2,1)}, u32[]{:S(2)}, u32[]{:S(2)}) %all-to-all-start.9) | async-done | bytes 524320 | tf_op jit(solution)/shard_map/all_to_all | solution.py:48
  437.4 2.3 pad_maximum_fusion.3
  440.8 99.4 %while.124 = (s32[]{:T(128)}, bf16[1,4096,128]{2,1,0:T(8,128)(2,1)}, bf16[1,4096,128]{2,1,0:T(8,128)(2,1)}, bf16[1,4096,128]{2,1,0:T(8,128)(2,1)S(1)}, f32[1,409...) while((s32[]{:T(128)}, bf16[1,4096,128]{2,1,0:T(8,128)(2,1)}, ...), condition=%wide.region_16.17_spmd, body=%wide.region_13.16_spmd.sunk | while | flops 135922688 | bytes 1856998 | solution.py:156
  441.7 19.2 %while.127 = (s32[]{:T(128)}, f32[1,512,128]{2,1,0:T(8,128)S(1)}, s32[]{:T(128)}, bf16[1,4096,128]{2,1,0:T(8,128)(2,1)S(1)}, bf16[1,512,128]{2,1,0:T(8,128)(2,1)...) while((s32[]{:T(128)}, f32[1,512,128]{2,1,0:T(8,128)S(1)}, ...), condition=%wide.region_15.15_spmd, body=%wide.region_14.14_spmd.sunk | while | flops 135857152 | bytes 939183 | solution.py:153
  462.6 16.8 %while.127 = (s32[]{:T(128)}, f32[1,512,128]{2,1,0:T(8,128)S(1)}, s32[]{:T(128)}, bf16[1,4096,128]{2,1,0:T(8,128)(2,1)S(1)}, bf16[1,512,128]{2,1,0:T(8,128)(2,1)...) while((s32[]{:T(128)}, f32[1,512,128]{2,1,0:T(8,128)S(1)}, ...), condition=%wide.region_15.15_spmd, body=%wide.region_14.14_spmd.sunk | while | flops 135857152 | bytes 939183 | solution.py:153
  481.0 14.4 %while.127 = (s32[]{:T(128)}, f32[1,512,128]{2,1,0:T(8,128)S(1)}, s32[]{:T(128)}, bf16[1,4096,128]{2,1,0:T(8,128)(2,1)S(1)}, bf16[1,512,128]{2,1,0:T(8,128)(2,1)...) while((s32[]{:T(128)}, f32[1,512,128]{2,1,0:T(8,128)S(1)}, ...), condition=%wide.region_15.15_spmd, body=%wide.region_14.14_spmd.sunk | while | flops 135857152 | bytes 939183 | solution.py:153
  497.0 12.0 %while.127 = (s32[]{:T(128)}, f32[1,512,128]{2,1,0:T(8,128)S(1)}, s32[]{:T(128)}, bf16[1,4096,128]{2,1,0:T(8,128)(2,1)S(1)}, bf16[1,512,128]{2,1,0:T(8,128)(2,1)...) while((s32[]{:T(128)}, f32[1,512,128]{2,1,0:T(8,128)S(1)}, ...), condition=%wide.region_15.15_spmd, body=%wide.region_14.14_spmd.sunk | while | flops 135857152 | bytes 939183 | solution.py:153
  510.6 9.6 %while.127 = (s32[]{:T(128)}, f32[1,512,128]{2,1,0:T(8,128)S(1)}, s32[]{:T(128)}, bf16[1,4096,128]{2,1,0:T(8,128)(2,1)S(1)}, bf16[1,512,128]{2,1,0:T(8,128)(2,1)...) while((s32[]{:T(128)}, f32[1,512,128]{2,1,0:T(8,128)S(1)}, ...), condition=%wide.region_15.15_spmd, body=%wide.region_14.14_spmd.sunk | while | flops 135857152 | bytes 939183 | solution.py:153
  521.9 7.2 %while.127 = (s32[]{:T(128)}, f32[1,512,128]{2,1,0:T(8,128)S(1)}, s32[]{:T(128)}, bf16[1,4096,128]{2,1,0:T(8,128)(2,1)S(1)}, bf16[1,512,128]{2,1,0:T(8,128)(2,1)...) while((s32[]{:T(128)}, f32[1,512,128]{2,1,0:T(8,128)S(1)}, ...), condition=%wide.region_15.15_spmd, body=%wide.region_14.14_spmd.sunk | while | flops 135857152 | bytes 939183 | solution.py:153
  530.7 4.8 while.127
  537.1 2.4 while.127
  540.2 4.3 copy.73
  545.0 23.4 %reduce.11 = bf16[4096,128]{1,0:T(8,128)(2,1)S(1)} reduce(bf16[4096,1,128]{2,1,0:T(2,128)(2,1)} %bitcast.194, bf16[]{:T(256)} %broadcast.149), dimensions={1}, to_apply=%bitcast.154.reduce_sub_computation | reduce | bytes 2097154
  569.6 30.6 %all_to_all.74 = bf16[32,2,8192]{2,1,0:T(2,128)(2,1)S(1)} all-to-all(bf16[32,2,8192]{2,1,0:T(2,128)(2,1)} %reshape.165), channel_id=1, replica_groups=mesh['seq'=32,'dp'=8] {'seq'}, dimensions={0} | all-to-all | bytes 2097152 | tf_op jit(solution)/shard_map/all_to_all | solution.py:217
  600.2 3.5 reshape.166
  606.1 29.7 %all_to_all.72 = bf16[8,1,128,1024]{2,3,1,0:T(8,128)(2,1)S(1)} all-to-all(bf16[8,1,128,1024]{2,3,1,0:T(8,128)(2,1)S(1)} %broadcast_in_dim.44), channel_id=1, replica_groups=mesh['seq'=32,'dp'=8] {'dp'}, dimensions={0} | all-to-all | bytes 4194304 | tf_op jit(solution)/shard_map/all_to_all | solution.py:54
  635.7 2.5 bitcast_convert_fusion
  638.2 33.2 %all_to_all.73 = bf16[32,32,512]{2,1,0:T(8,128)(2,1)S(1)} all-to-all(bf16[32,32,512]{2,1,0:T(8,128)(2,1)S(1)} %bitcast.211), channel_id=1, replica_groups=mesh['seq'=32,'dp'=8] {'seq'}, dimensions={0} | all-to-all | bytes 2097152 | tf_op jit(solution)/shard_map/all_to_all | solution.py:25
  (538 shorter events, 263.4 us)
Async XLA Ops:
  0.6 393.5 %copy-start = (bf16[4096,256]{1,0:T(8,128)(2,1)S(1)}, bf16[4096,256]{1,0:T(8,128)(2,1)}, u32[]{:S(2)}) copy-start(bf16[4096,256]{1,0:T(8,128)(2,1)} %param.24) | copy-start | bytes 6291460
  13.3 20.3 %all-to-all-start = ((bf16[8,1,128,512]{3,2,1,0:T(8,128)(2,1)}), bf16[8,1,128,512]{3,2,1,0:T(8,128)(2,1)}, u32[]{:S(2)}, u32[]{:S(2)}) async-start(bf16[8,1,128,512]{3,2,1,0:T(8,128)(2,1)} %bitcast_dynamic-update-slice_fusion), calls=%async_computation | async-start | bytes 2097152 | tf_op jit(solution)/shard_map/all_to_all | solution.py:14
  21.0 24.4 %copy-start.6 = (bf16[512,1024]{1,0:T(8,128)(2,1)S(1)}, bf16[512,1024]{1,0:T(8,128)(2,1)}, u32[]{:S(2)}) copy-start(bf16[512,1024]{1,0:T(8,128)(2,1)} %param.23) | copy-start | bytes 3145732
  33.6 28.3 %all-to-all-start.4 = ((bf16[32,1,64,128]{3,2,1,0:T(8,128)(2,1)}), bf16[32,1,64,128]{3,2,1,0:T(8,128)(2,1)}, u32[]{:S(2)}, u32[]{:S(2)}) async-start(bf16[32,1,64,128]{3,2,1,0:T(8,128)(2,1)} %copy.51), calls=%async_computation.4 | async-start | bytes 1048576 | tf_op jit(solution)/shard_map/all_to_all | solution.py:48
  49.2 17.1 %copy-start.1 = (bf16[32,1,64,128]{2,3,0,1:T(8,128)(2,1)S(1)}, bf16[32,1,64,128]{2,3,0,1:T(8,128)(2,1)}, u32[]{:S(2)}) copy-start(bf16[32,1,64,128]{2,3,0,1:T(8,128)(2,1)} %get-tuple-element.823) | copy-start | bytes 1572868
  62.0 31.5 %all-to-all-start.1 = ((bf16[8,1,128,1024]{3,2,1,0:T(8,128)(2,1)}), bf16[8,1,128,1024]{3,2,1,0:T(8,128)(2,1)}, u32[]{:S(2)}, u32[]{:S(2)}) async-start(bf16[8,1,128,1024]{3,2,1,0:T(8,128)(2,1)} %convert_bitcast_fusion), calls=%async_computation.1 | async-start | bytes 4194304 | tf_op jit(solution)/shard_map/all_to_all | solution.py:25
  66.3 32.8 %copy-start.2 = (bf16[1,128,1024]{2,1,0:T(8,128)(2,1)S(1)}, bf16[1,128,1024]{2,1,0:T(8,128)(2,1)}, u32[]{:S(2)}) copy-start(bf16[1,128,1024]{2,1,0:T(8,128)(2,1)} %param.21) | copy-start | bytes 786436
  93.5 22.3 %all-to-all-start.5 = ((bf16[32,1,64,128]{3,2,1,0:T(8,128)(2,1)}), bf16[32,1,64,128]{3,2,1,0:T(8,128)(2,1)}, u32[]{:S(2)}, u32[]{:S(2)}) async-start(bf16[32,1,64,128]{3,2,1,0:T(8,128)(2,1)} %copy.52), calls=%async_computation.5 | async-start | bytes 1048576 | tf_op jit(solution)/shard_map/all_to_all | solution.py:48
  148.4 32.4 %all-to-all-start.3 = ((bf16[32,1,64,256]{3,2,1,0:T(8,128)(2,1)}), bf16[32,1,64,256]{3,2,1,0:T(8,128)(2,1)}, u32[]{:S(2)}, u32[]{:S(2)}) async-start(bf16[32,1,64,256]{3,2,1,0:T(8,128)(2,1)} %get-tuple-element.817), calls=%async_computation.3 | async-start | bytes 2097152 | tf_op jit(solution)/shard_map/all_to_all | solution.py:48
  368.7 20.8 %all-to-all-start.7 = ((bf16[32,1,64,128]{3,2,1,0:T(8,128)(2,1)}), bf16[32,1,64,128]{3,2,1,0:T(8,128)(2,1)}, u32[]{:S(2)}, u32[]{:S(2)}) async-start(bf16[32,1,64,128]{3,2,1,0:T(8,128)(2,1)} %get-tuple-element.821), calls=%async_computation.7 | async-start | bytes 1048576 | tf_op jit(solution)/shard_map/all_to_all | solution.py:48
  376.8 17.4 %copy-start.3 = (f32[1,128,256]{2,1,0:T(8,128)S(1)}, f32[1,128,256]{2,1,0:T(8,128)}, u32[]{:S(2)}) copy-start(f32[1,128,256]{2,1,0:T(8,128)} %param.25) | copy-start | bytes 393220
  394.1 0.8 copy-start.5
  417.5 19.8 %all-to-all-start.9 = ((bf16[32,1,64,128]{3,2,1,0:T(8,128)(2,1)}), bf16[32,1,64,128]{3,2,1,0:T(8,128)(2,1)}, u32[]{:S(2)}, u32[]{:S(2)}) async-start(bf16[32,1,64,128]{3,2,1,0:T(8,128)(2,1)} %get-tuple-element.819), calls=%async_computation.9 | async-start | bytes 1048576 | tf_op jit(solution)/shard_map/all_to_all | solution.py:48
  638.2 33.4 %copy-start.4 = (f32[32,512]{1,0:T(8,128)S(1)}, f32[32,512]{1,0:T(8,128)}, u32[]{:S(2)}) copy-start(f32[32,512]{1,0:T(8,128)} %param.27) | copy-start | bytes 196612
